TPU v7x, 256 devices: a whole 4x4x8 slice. The times are simulated.
256 devices in a mesh: slab: 64 (over x, y, z_hi), col: 4 (over z_lo, core).
Axes of the slice: x: 4, y: 4, z: 8 (z_hi: 4, z_lo: 2; z = z_hi * 2 + z_lo), core: 2. Of those that a mesh axis runs over, the one named last changes fastest.
Arguments:
- psi0: bfloat16 [256, 256, 1024], P('col', 'slab'), may hold values from -4 to 4
- onsite: float32 [256, 1024], P('slab'), may hold values from -0.4 to 0.4
- hop_x: float32 [256, 1024], P('slab'), may hold values from 0.12 to 0.36
- hop_y: float32 [256, 1024], P('slab'), may hold values from 0.12 to 0.36
- cos_coef: float32 [8, 3], replicated, may hold values from -1 to 1
- sin_coef: float32 [8, 3], replicated, may hold values from -1 to 1
Outputs:
- currents: float32 [8, 2, 256, 1024], P(None, None, 'slab', 'col')
All inputs are finite; a program needn't handle non-finite values.
Results may differ from a plain program's by a relative error of at most 0.0051.
Values may be sent and summed in bfloat16 or wider, within the bound.
A program may use at most 128 MiB of HBM per device.

v0:
```python
import functools

import jax
import jax.numpy as jnp
from jax import lax
from jax.experimental import pallas as pl
from jax.experimental.pallas import tpu as pltpu
from jax.sharding import PartitionSpec as P

MESH = pl.DeviceIdType.MESH
CHUNKS = 8
STEP = 2


def kernel(slabs, cols, psi, onsite, hop_x, hop_y, cos_ref, sin_ref, out,
           field, to_up, to_down, from_down, from_up, coef, acc, part, extra,
           got, got_extra, local_sem, send_sem, recv_sem, coef_send, coef_recv,
           part_send, part_recv, extra_send, extra_recv):
    slab = lax.axis_index("slab")
    col = lax.axis_index("col")
    batch, rows, width = psi.shape
    per = batch // CHUNKS
    quarter = width // cols
    has_down = slab > 0
    has_up = slab < slabs - 1

    def span(i):
        return pl.ds(i * per, per)

    def local(i):
        return pltpu.make_async_copy(
            psi.at[span(i)], field.at[span(i), 2:6, :], local_sem.at[i])

    def upward(i):
        return pltpu.make_async_remote_copy(
            src_ref=psi.at[span(i), 2:4, :], dst_ref=field.at[span(i), 0:2, :],
            send_sem=send_sem.at[0, i], recv_sem=recv_sem.at[0, i],
            device_id=(slab + 1, col), device_id_type=MESH)

    def downward(i):
        return pltpu.make_async_remote_copy(
            src_ref=psi.at[span(i), 0:2, :], dst_ref=field.at[span(i), 6:8, :],
            send_sem=send_sem.at[1, i], recv_sem=recv_sem.at[1, i],
            device_id=(slab - 1, col), device_id_type=MESH)

    coef_up = pltpu.make_async_remote_copy(
        src_ref=to_up, dst_ref=from_down, send_sem=coef_send.at[0],
        recv_sem=coef_recv.at[0], device_id=(slab + 1, col), device_id_type=MESH)
    coef_down = pltpu.make_async_remote_copy(
        src_ref=to_down, dst_ref=from_up, send_sem=coef_send.at[1],
        recv_sem=coef_recv.at[1], device_id=(slab - 1, col), device_id_type=MESH)

    for i in range(CHUNKS):
        local(i).start()

    barrier = pltpu.get_barrier_semaphore()
    for by in range(1, cols):
        pl.semaphore_signal(barrier, inc=1, device_id=(slab, lax.rem(col + by, cols)),
                            device_id_type=MESH)

    @pl.when(has_up)
    def _():
        for other in range(cols):
            pl.semaphore_signal(barrier, inc=1, device_id=(slab + 1, other), device_id_type=MESH)

    @pl.when(has_down)
    def _():
        for other in range(cols):
            pl.semaphore_signal(barrier, inc=1, device_id=(slab - 1, other), device_id_type=MESH)

    zero = jnp.zeros((1, width), jnp.float32)
    to_up[...] = jnp.concatenate(
        [hop_x[2:4, :], onsite[3:4, :], hop_y[3:4, :]], axis=0)
    to_down[...] = jnp.concatenate(
        [hop_x[0:1, :], onsite[0:1, :], hop_y[0:1, :], zero], axis=0)

    sides = jnp.where(has_up, 1, 0) + jnp.where(has_down, 1, 0)
    pl.semaphore_wait(barrier, cols - 1 + cols * sides)

    @pl.when(has_up)
    def _():
        coef_up.start()

    @pl.when(has_down)
    def _():
        coef_down.start()

    for i in range(CHUNKS):
        @pl.when(has_up)
        def _():
            upward(i).start()

        @pl.when(has_down)
        def _():
            downward(i).start()

    blank = jnp.zeros((batch, 2, width), jnp.bfloat16)

    @pl.when(jnp.logical_not(has_down))
    def _():
        field[:, 0:2, :] = blank
        from_down[...] = jnp.zeros_like(from_down)

    @pl.when(jnp.logical_not(has_up))
    def _():
        field[:, 6:8, :] = blank
        from_up[...] = jnp.zeros_like(from_up)

    acc[...] = jnp.zeros_like(acc)

    @pl.when(has_down)
    def _():
        coef_up.wait_recv()

    @pl.when(has_up)
    def _():
        coef_down.wait_recv()

    low = from_down[...]
    high = from_up[...]
    site_x = jnp.concatenate([low[0:2], hop_x[...], high[0:1], zero], axis=0)
    site_on = jnp.concatenate([zero, low[2:3], onsite[...], high[1:2], zero], axis=0)
    site_y = jnp.concatenate([zero, low[3:4], hop_y[...], high[2:3], zero], axis=0)
    row_id = lax.broadcasted_iota(jnp.int32, (8, width), 0)
    lane_id = lax.broadcasted_iota(jnp.int32, (8, width), 1)
    even = lax.rem(row_id + lane_id, 2) == 0
    site_x = jnp.where((row_id == 5) & jnp.logical_not(has_up), 0.0, site_x)
    bond_y = jnp.where(even & (lane_id < width - 1), site_y, 0.0)
    coef[0] = site_on
    coef[1] = pltpu.roll(site_x, 1, 0)
    coef[2] = site_x
    coef[3] = bond_y + pltpu.roll(bond_y, 1, 1)

    def partner(f):
        return jnp.where(even, pltpu.roll(f, width - 1, 1), pltpu.roll(f, 1, 1))

    def hamiltonian(f, above, beside):
        return coef[0] * f - coef[1] * pltpu.roll(f, 1, 0) - coef[2] * above - coef[3] * beside

    def one(c):
        p = field[c].astype(jnp.float32)
        p_up = pltpu.roll(p, 7, 0)
        p_side = partner(p)
        q = hamiltonian(p, p_up, p_side).astype(jnp.bfloat16).astype(jnp.float32)
        q_up = pltpu.roll(q, 7, 0)
        q_side = partner(q)
        t = (2.0 * hamiltonian(q, q_up, q_side) - p).astype(jnp.bfloat16).astype(jnp.float32)
        t_up = pltpu.roll(t, 7, 0)
        t_side = partner(t)
        return (
            p * q_up - q * p_up, p * t_up, t * p_up, q * t_up, t * q_up,
            p * q_side - q * p_side, p * t_side - t * p_side, q * t_side - t * q_side)

    def chunk(i, carry):
        local(i).wait()

        @pl.when(has_down)
        def _():
            upward(i).wait_recv()

        @pl.when(has_up)
        def _():
            downward(i).wait_recv()

        def columns(j, inner):
            first = i * per + j * STEP
            terms = one(first)
            for k in range(1, STEP):
                terms = [a + b for a, b in zip(terms, one(first + k))]
            for n, term in enumerate(terms):
                acc[n] += term
            return inner

        return lax.fori_loop(0, per // STEP, columns, carry)

    lax.fori_loop(0, CHUNKS, chunk, 0)

    first_half = row_id < 4

    def packed(along, across):
        return jnp.where(first_half, pltpu.roll(along, 6, 0), pltpu.roll(across, 2, 0))

    top = row_id == 5
    whole = (
        packed(acc[0], acc[5]),
        packed(jnp.where(top, 0.0, acc[1]) - acc[2], acc[6]),
        packed(jnp.where(top, 0.0, acc[3]) - acc[4], acc[7]))
    for k in range(3):
        for j in range(cols):
            part[j, k] = whole[k][:, j * quarter:(j + 1) * quarter]
    two = jnp.concatenate([acc[1, 1:2, :], acc[3, 1:2, :]], axis=0)
    for j in range(cols):
        extra[j] = two[:, j * quarter:(j + 1) * quarter]

    def to_peer(by):
        peer = lax.rem(col + by, cols)
        return pltpu.make_async_remote_copy(
            src_ref=part.at[peer], dst_ref=got.at[by - 1], send_sem=part_send.at[by - 1],
            recv_sem=part_recv.at[by - 1], device_id=(slab, peer), device_id_type=MESH)

    def to_below(by):
        peer = lax.rem(col + by, cols)
        return pltpu.make_async_remote_copy(
            src_ref=extra.at[peer], dst_ref=got_extra.at[by], send_sem=extra_send.at[by],
            recv_sem=extra_recv.at[by], device_id=(slab - 1, peer), device_id_type=MESH)

    for by in range(1, cols):
        to_peer(by).start()

    @pl.when(has_down)
    def _():
        for by in range(cols):
            to_below(by).start()

    @pl.when(jnp.logical_not(has_up))
    def _():
        got_extra[...] = jnp.zeros_like(got_extra)

    for by in range(1, cols):
        to_peer(by).wait_recv()

    @pl.when(has_up)
    def _():
        for by in range(cols):
            to_below(by).wait_recv()

    here = pl.ds(pl.multiple_of(col * quarter, quarter), quarter)
    extra_sum = got_extra[0] + got_extra[1] + got_extra[2] + got_extra[3]
    own_x = hop_x[:, here]
    own_y = hop_y[:, here]
    row4 = lax.broadcasted_iota(jnp.int32, (4, quarter), 0)
    lane4 = lax.broadcasted_iota(jnp.int32, (4, quarter), 1)
    keep = (lax.rem(row4 + lane4, 2) == 0) & (lane4 + col * quarter < width - 1)
    own_y = jnp.where(keep, own_y, 0.0)
    along = []
    across = []
    for k in range(3):
        total = part[col, k] + got[0, k] + got[1, k] + got[2, k]
        a = total[0:4]
        if k:
            a = a + jnp.where(row4 == 3, extra_sum[k - 1:k], 0.0)
        along.append(a * own_x)
        across.append(total[4:8] * own_y)
    for e in range(cos_ref.shape[1]):
        c0, c1, c2 = (cos_ref[n, e] for n in range(3))
        s0, s1, s2 = (sin_ref[n, e] for n in range(3))
        d = (c0 * s1 - c1 * s0, c0 * s2 - c2 * s0, c1 * s2 - c2 * s1)
        out[e, 0] = d[0] * along[0] + d[1] * along[1] + d[2] * along[2]
        out[e, 1] = d[0] * across[0] + d[1] * across[1] + d[2] * across[2]

    @pl.when(has_up)
    def _():
        coef_up.wait_send()
        for i in range(CHUNKS):
            upward(i).wait_send()

    @pl.when(has_down)
    def _():
        coef_down.wait_send()
        for i in range(CHUNKS):
            downward(i).wait_send()
        for by in range(cols):
            to_below(by).wait_send()

    for by in range(1, cols):
        to_peer(by).wait_send()


def solution(mesh):
    slabs, cols = mesh.shape["slab"], mesh.shape["col"]

    def on_device(psi0, onsite, hop_x, hop_y, cos_coef, sin_coef):
        batch, rows, width = psi0.shape
        quarter = width // cols
        vmem = pl.BlockSpec(memory_space=pltpu.VMEM)
        smem = pl.BlockSpec(memory_space=pltpu.SMEM)
        f32 = jnp.float32
        return pl.pallas_call(
            functools.partial(kernel, slabs, cols),
            out_shape=jax.ShapeDtypeStruct((cos_coef.shape[0], 2, rows, quarter), f32),
            in_specs=[pl.BlockSpec(memory_space=pl.ANY), vmem, vmem, vmem, smem, smem],
            out_specs=vmem,
            scratch_shapes=[
                pltpu.VMEM((batch, 8, width), jnp.bfloat16),
                pltpu.VMEM((4, width), f32),
                pltpu.VMEM((4, width), f32),
                pltpu.VMEM((4, width), f32),
                pltpu.VMEM((4, width), f32),
                pltpu.VMEM((4, 8, width), f32),
                pltpu.VMEM((8, 8, width), f32),
                pltpu.VMEM((cols, 3, 8, quarter), f32),
                pltpu.VMEM((cols, 2, quarter), f32),
                pltpu.VMEM((cols - 1, 3, 8, quarter), f32),
                pltpu.VMEM((cols, 2, quarter), f32),
                pltpu.SemaphoreType.DMA((CHUNKS,)),
                pltpu.SemaphoreType.DMA((2, CHUNKS)),
                pltpu.SemaphoreType.DMA((2, CHUNKS)),
                pltpu.SemaphoreType.DMA((2,)),
                pltpu.SemaphoreType.DMA((2,)),
                pltpu.SemaphoreType.DMA((cols - 1,)),
                pltpu.SemaphoreType.DMA((cols - 1,)),
                pltpu.SemaphoreType.DMA((cols,)),
                pltpu.SemaphoreType.DMA((cols,)),
            ],
            compiler_params=pltpu.CompilerParams(
                collective_id=0, has_side_effects=True, vmem_limit_bytes=32 << 20),
        )(psi0, onsite, hop_x, hop_y, cos_coef.T, sin_coef.T)

    placed = (P("col", "slab", None), P("slab", None), P("slab", None), P("slab", None), P(), P())
    return jax.shard_map(
        on_device,
        mesh=mesh,
        in_specs=placed,
        out_specs=P(None, None, "slab", "col"),
        check_vma=False,
    )
```

profile of v0, /device:TPU:7, one launch (start us, length us, event | category | flops | bytes accessed | tf_op | source)
XLA Modules:
  0.0 38.4 jit_solution(8520519026362509524)
XLA Ops:
  0.0 0.0 copy-start.4
  0.0 0.7 %copy-done.4 = f32[8,3]{0,1:T(4,128)S(1)} copy-done((f32[8,3]{0,1:T(4,128)S(1)}, f32[8,3]{0,1:T(4,128)}, u32[]{:S(2)}) %copy-start.4) | copy-done | bytes 120
  0.7 0.0 copy-start
  0.7 1.0 %copy-done = bf16[64,4,1024]{2,1,0:T(4,128)(2,1)S(1)} copy-done((bf16[64,4,1024]{2,1,0:T(4,128)(2,1)S(1)}, bf16[64,4,1024]{2,1,0:T(4,128)(2,1)}, u32[]{:S(2)}) %copy-start) | copy-done | bytes 524312
  1.7 0.0 copy-start.1
  1.7 0.7 %copy-done.1 = f32[4,1024]{1,0:T(4,128)S(1)} copy-done((f32[4,1024]{1,0:T(4,128)S(1)}, f32[4,1024]{1,0:T(4,128)}, u32[]{:S(2)}) %copy-start.1) | copy-done | bytes 16408
  2.4 0.0 copy-start.2
  2.4 0.7 %copy-done.2 = f32[4,1024]{1,0:T(4,128)S(1)} copy-done((f32[4,1024]{1,0:T(4,128)S(1)}, f32[4,1024]{1,0:T(4,128)}, u32[]{:S(2)}) %copy-start.2) | copy-done | bytes 16408
  3.2 0.0 copy-start.3
  3.2 0.7 %copy-done.3 = f32[4,1024]{1,0:T(4,128)S(1)} copy-done((f32[4,1024]{1,0:T(4,128)S(1)}, f32[4,1024]{1,0:T(4,128)}, u32[]{:S(2)}) %copy-start.3) | copy-done | bytes 16408
  3.9 0.0 copy-start.5
  3.9 0.7 %copy-done.5 = f32[8,3]{0,1:T(4,128)S(1)} copy-done((f32[8,3]{0,1:T(4,128)S(1)}, f32[8,3]{0,1:T(4,128)}, u32[]{:S(2)}) %copy-start.5) | copy-done | bytes 120
  4.6 33.2 %shard_map.64 = f32[8,2,4,256]{3,2,1,0:T(4,128)S(1)} custom-call(bf16[64,4,1024]{2,1,0:T(4,128)(2,1)S(1)} %copy-done, f32[4,1024]{1,0:T(4,128)S(1)} %copy-done.1, f32[4,1024]{1,0:T(4,128)S(1)} %copy-done.2, f32[4,1024]{1,0:T(4,128)S(1)} %copy-done.3, f32[3,8]{1,0:T(4,128)S(1)} %bitcast.2, f32[3,8]{1,0:T(4,128)S(1)} %bitcast.3), custom_call_target="tpu_custom_call" | custom-call | tf_op jit(solution)/shard_map/pallas_call | solution.py:278
  37.8 0.6 %copy.8 = f32[8,2,4,256]{3,2,1,0:T(4,128)} copy(f32[8,2,4,256]{3,2,1,0:T(4,128)S(1)} %shard_map.64) | data formatting | bytes 131072
Async XLA Ops:
  0.0 0.7 %copy-start.4 = (f32[8,3]{0,1:T(4,128)S(1)}, f32[8,3]{0,1:T(4,128)}, u32[]{:S(2)}) copy-start(f32[8,3]{0,1:T(4,128)} %param.10) | copy-start | bytes 292
  0.7 1.0 %copy-start = (bf16[64,4,1024]{2,1,0:T(4,128)(2,1)S(1)}, bf16[64,4,1024]{2,1,0:T(4,128)(2,1)}, u32[]{:S(2)}) copy-start(bf16[64,4,1024]{2,1,0:T(4,128)(2,1)} %psi.1) | copy-start | bytes 1572868
  1.7 0.7 %copy-start.1 = (f32[4,1024]{1,0:T(4,128)S(1)}, f32[4,1024]{1,0:T(4,128)}, u32[]{:S(2)}) copy-start(f32[4,1024]{1,0:T(4,128)} %onsite.1) | copy-start | bytes 49156
  2.4 0.7 %copy-start.2 = (f32[4,1024]{1,0:T(4,128)S(1)}, f32[4,1024]{1,0:T(4,128)}, u32[]{:S(2)}) copy-start(f32[4,1024]{1,0:T(4,128)} %hop_x.1) | copy-start | bytes 49156
  3.2 0.7 %copy-start.3 = (f32[4,1024]{1,0:T(4,128)S(1)}, f32[4,1024]{1,0:T(4,128)}, u32[]{:S(2)}) copy-start(f32[4,1024]{1,0:T(4,128)} %hop_y.1) | copy-start | bytes 49156
  3.9 0.7 %copy-start.5 = (f32[8,3]{0,1:T(4,128)S(1)}, f32[8,3]{0,1:T(4,128)}, u32[]{:S(2)}) copy-start(f32[8,3]{0,1:T(4,128)} %param.11) | copy-start | bytes 292
where the time goes:
time: 38.8 us; the launch traced here: 38.4 us
  Pallas kernels  33.2 us (86%)
  local copies, waits for them, and re-layouts  5.19 us (13%)
    pallas_call x1, Pallas kernels, on_device(): pl.pallas_call(functools.partial(kernel, slabs, cols), out_shape=jax.Shap...  33.2 us
    unnamed x13, local copies, waits for them, and re-layouts  5.19 us

commit v1 on v0

--- a/solution.py
+++ b/solution.py
@@ -9,11 +9,11 @@
 
 MESH = pl.DeviceIdType.MESH
 CHUNKS = 8
-STEP = 2
-
-
-def kernel(slabs, cols, psi, onsite, hop_x, hop_y, cos_ref, sin_ref, out,
-           field, to_up, to_down, from_down, from_up, coef, acc, part, extra,
+LANES = 128
+
+
+def kernel(slabs, cols, psi, onsite_hbm, hop_x_hbm, hop_y_hbm, cos_hbm, sin_hbm, out,
+           onsite, hop_x, hop_y, cos_ref, sin_ref, input_sem, field, to_up, to_down, from_down, from_up, coef, states, first, second, beside, acc, part, extra,
            got, got_extra, local_sem, send_sem, recv_sem, coef_send, coef_recv,
            part_send, part_recv, extra_send, extra_recv):
     slab = lax.axis_index("slab")
@@ -50,6 +50,13 @@
         src_ref=to_down, dst_ref=from_up, send_sem=coef_send.at[1],
         recv_sem=coef_recv.at[1], device_id=(slab - 1, col), device_id_type=MESH)
 
+    loads = [
+        pltpu.make_async_copy(source, target, input_sem.at[n])
+        for n, (source, target) in enumerate((
+            (hop_x_hbm, hop_x), (onsite_hbm, onsite), (hop_y_hbm, hop_y),
+            (cos_hbm, cos_ref), (sin_hbm, sin_ref)))]
+    for load in loads:
+        load.start()
     for i in range(CHUNKS):
         local(i).start()
 
@@ -68,6 +75,8 @@
         for other in range(cols):
             pl.semaphore_signal(barrier, inc=1, device_id=(slab - 1, other), device_id_type=MESH)
 
+    for load in loads:
+        load.wait()
     zero = jnp.zeros((1, width), jnp.float32)
     to_up[...] = jnp.concatenate(
         [hop_x[2:4, :], onsite[3:4, :], hop_y[3:4, :]], axis=0)
@@ -123,33 +132,54 @@
     site_y = jnp.concatenate([zero, low[3:4], hop_y[...], high[2:3], zero], axis=0)
     row_id = lax.broadcasted_iota(jnp.int32, (8, width), 0)
     lane_id = lax.broadcasted_iota(jnp.int32, (8, width), 1)
-    even = lax.rem(row_id + lane_id, 2) == 0
     site_x = jnp.where((row_id == 5) & jnp.logical_not(has_up), 0.0, site_x)
-    bond_y = jnp.where(even & (lane_id < width - 1), site_y, 0.0)
-    coef[0] = site_on
-    coef[1] = pltpu.roll(site_x, 1, 0)
-    coef[2] = site_x
-    coef[3] = bond_y + pltpu.roll(bond_y, 1, 1)
-
-    def partner(f):
-        return jnp.where(even, pltpu.roll(f, width - 1, 1), pltpu.roll(f, 1, 1))
-
-    def hamiltonian(f, above, beside):
-        return coef[0] * f - coef[1] * pltpu.roll(f, 1, 0) - coef[2] * above - coef[3] * beside
-
-    def one(c):
-        p = field[c].astype(jnp.float32)
-        p_up = pltpu.roll(p, 7, 0)
-        p_side = partner(p)
-        q = hamiltonian(p, p_up, p_side).astype(jnp.bfloat16).astype(jnp.float32)
-        q_up = pltpu.roll(q, 7, 0)
-        q_side = partner(q)
-        t = (2.0 * hamiltonian(q, q_up, q_side) - p).astype(jnp.bfloat16).astype(jnp.float32)
-        t_up = pltpu.roll(t, 7, 0)
-        t_side = partner(t)
-        return (
-            p * q_up - q * p_up, p * t_up, t * p_up, q * t_up, t * q_up,
-            p * q_side - q * p_side, p * t_side - t * p_side, q * t_side - t * q_side)
+    bond_y = jnp.where((lax.rem(row_id + lane_id, 2) == 0) & (lane_id < width - 1), site_y, 0.0)
+    both_y = bond_y + pltpu.roll(bond_y, 1, 1)
+    for x in range(8):
+        coef[0, x] = jnp.broadcast_to(site_on[x:x + 1], (8, width))
+        coef[1, x] = jnp.broadcast_to(site_x[x:x + 1], (8, width))
+        coef[2, x] = jnp.broadcast_to(both_y[x:x + 1], (8, width))
+
+    lane = lax.broadcasted_iota(jnp.int32, (8, LANES), 1)
+    odd_lane = lax.rem(lane, 2)
+    near = (lane + 1 - 2 * odd_lane, lax.rem(lane + LANES - 1 + 2 * odd_lane, LANES))
+    first_lane = lane == 0
+    last_lane = lane == LANES - 1
+    even_lane = odd_lane == 0
+    tiles = width // LANES
+
+    def partner(f, x):
+        parts = [
+            jnp.take_along_axis(f[:, k * LANES:(k + 1) * LANES], near[x % 2], axis=1)
+            for k in range(tiles)]
+        if x % 2:
+            parts = [
+                jnp.where(last_lane, parts[(k + 1) % tiles],
+                          jnp.where(first_lane, parts[k - 1], parts[k]))
+                for k in range(tiles)]
+        return jnp.concatenate(parts, axis=1)
+
+    def rounded(f):
+        return f.astype(jnp.bfloat16).astype(jnp.float32)
+
+    def mixed(f, g):
+        return jnp.concatenate([
+            jnp.where(even_lane, f[:, k * LANES:(k + 1) * LANES], g[:, k * LANES:(k + 1) * LANES])
+            for k in range(tiles)], axis=1)
+
+    def p_row(x):
+        return jnp.concatenate(
+            [states[k, pl.ds(x + 2, 8, stride=8), :] for k in range(tiles)], axis=1)
+
+    def hamiltonian(row, x, side):
+        return (coef[0, x + 2] * row(x) - coef[1, x + 1] * row(x - 1)
+                - coef[1, x + 2] * row(x + 1) - coef[2, x + 2] * side)
+
+    def q_row(x):
+        return first[x + 1]
+
+    def t_row(x):
+        return second[x]
 
     def chunk(i, carry):
         local(i).wait()
@@ -162,33 +192,63 @@
         def _():
             downward(i).wait_recv()
 
-        def columns(j, inner):
-            first = i * per + j * STEP
-            terms = one(first)
-            for k in range(1, STEP):
-                terms = [a + b for a, b in zip(terms, one(first + k))]
-            for n, term in enumerate(terms):
-                acc[n] += term
+        def group(j, inner):
+            for c in range(8):
+                block = field[i * per + j * 8 + c].astype(jnp.float32)
+                for k in range(tiles):
+                    states[k, 8 * c:8 * c + 8, :] = block[:, k * LANES:(k + 1) * LANES]
+            for x in range(-1, rows + 1):
+                side = partner(p_row(x), x)
+                if 0 <= x < rows:
+                    beside[0, x] = side
+                first[x + 1] = rounded(hamiltonian(p_row, x, side))
+            for x in range(rows):
+                side = partner(q_row(x), x)
+                beside[1, x] = side
+                t = rounded(2.0 * hamiltonian(q_row, x, side) - p_row(x))
+                second[x] = t
+                beside[2, x] = partner(t, x)
+            for x in range(rows):
+                acc[x] += p_row(x) * q_row(x + 1) - q_row(x) * p_row(x + 1)
+                if x < rows - 1:
+                    acc[8 + x] += p_row(x) * t_row(x + 1) - t_row(x) * p_row(x + 1)
+                    acc[16 + x] += q_row(x) * t_row(x + 1) - t_row(x) * q_row(x + 1)
+                else:
+                    acc[8 + x] -= t_row(x) * p_row(x + 1)
+                    acc[16 + x] -= t_row(x) * q_row(x + 1)
+            acc[14] += p_row(-1) * t_row(0)
+            acc[22] += q_row(-1) * t_row(0)
+            for h in range(rows // 2):
+                x = 2 * h
+                own = (mixed(p_row(x), p_row(x + 1)), mixed(q_row(x), q_row(x + 1)),
+                       mixed(t_row(x), t_row(x + 1)))
+                side = [mixed(beside[n, x], beside[n, x + 1]) for n in range(3)]
+                acc[4 + h] += own[0] * side[1] - own[1] * side[0]
+                acc[12 + h] += own[0] * side[2] - own[2] * side[0]
+                acc[20 + h] += own[1] * side[2] - own[2] * side[1]
             return inner
 
-        return lax.fori_loop(0, per // STEP, columns, carry)
+        return lax.fori_loop(0, per // 8, group, carry)
 
     lax.fori_loop(0, CHUNKS, chunk, 0)
 
-    first_half = row_id < 4
-
-    def packed(along, across):
-        return jnp.where(first_half, pltpu.roll(along, 6, 0), pltpu.roll(across, 2, 0))
-
-    top = row_id == 5
-    whole = (
-        packed(acc[0], acc[5]),
-        packed(jnp.where(top, 0.0, acc[1]) - acc[2], acc[6]),
-        packed(jnp.where(top, 0.0, acc[3]) - acc[4], acc[7]))
+    def folded(maps):
+        size = 4
+        while size:
+            upper = lax.rem(row_id // size, 2) == 1
+            half = len(maps) // 2
+            maps = [
+                jnp.where(upper, maps[n + half] + pltpu.roll(maps[n + half], size, 0),
+                          maps[n] + pltpu.roll(maps[n], 8 - size, 0))
+                for n in range(half)]
+            size //= 2
+        return maps[0]
+
+    whole = [folded([acc[8 * k + n] for n in range(8)]) for k in range(3)]
     for k in range(3):
         for j in range(cols):
             part[j, k] = whole[k][:, j * quarter:(j + 1) * quarter]
-    two = jnp.concatenate([acc[1, 1:2, :], acc[3, 1:2, :]], axis=0)
+    two = jnp.concatenate([whole[1][6:7], whole[2][6:7]], axis=0)
     for j in range(cols):
         extra[j] = two[:, j * quarter:(j + 1) * quarter]
 
@@ -240,7 +300,7 @@
         if k:
             a = a + jnp.where(row4 == 3, extra_sum[k - 1:k], 0.0)
         along.append(a * own_x)
-        across.append(total[4:8] * own_y)
+        across.append(jnp.concatenate([total[4:5], total[4:5], total[5:6], total[5:6]], axis=0) * own_y)
     for e in range(cos_ref.shape[1]):
         c0, c1, c2 = (cos_ref[n, e] for n in range(3))
         s0, s1, s2 = (sin_ref[n, e] for n in range(3))
@@ -273,21 +333,31 @@
         batch, rows, width = psi0.shape
         quarter = width // cols
         vmem = pl.BlockSpec(memory_space=pltpu.VMEM)
-        smem = pl.BlockSpec(memory_space=pltpu.SMEM)
+        hbm = pl.BlockSpec(memory_space=pltpu.HBM)
         f32 = jnp.float32
         return pl.pallas_call(
             functools.partial(kernel, slabs, cols),
             out_shape=jax.ShapeDtypeStruct((cos_coef.shape[0], 2, rows, quarter), f32),
-            in_specs=[pl.BlockSpec(memory_space=pl.ANY), vmem, vmem, vmem, smem, smem],
+            in_specs=[hbm] * 6,
             out_specs=vmem,
             scratch_shapes=[
+                pltpu.VMEM((rows, width), f32),
+                pltpu.VMEM((rows, width), f32),
+                pltpu.VMEM((rows, width), f32),
+                pltpu.SMEM(cos_coef.shape[::-1], f32),
+                pltpu.SMEM(sin_coef.shape[::-1], f32),
+                pltpu.SemaphoreType.DMA((5,)),
                 pltpu.VMEM((batch, 8, width), jnp.bfloat16),
                 pltpu.VMEM((4, width), f32),
                 pltpu.VMEM((4, width), f32),
                 pltpu.VMEM((4, width), f32),
                 pltpu.VMEM((4, width), f32),
-                pltpu.VMEM((4, 8, width), f32),
-                pltpu.VMEM((8, 8, width), f32),
+                pltpu.VMEM((3, 8, 8, width), f32),
+                pltpu.VMEM((width // LANES, 64, LANES), f32),
+                pltpu.VMEM((rows + 2, 8, width), f32),
+                pltpu.VMEM((rows, 8, width), f32),
+                pltpu.VMEM((3, rows, 8, width), f32),
+                pltpu.VMEM((24, 8, width), f32),
                 pltpu.VMEM((cols, 3, 8, quarter), f32),
                 pltpu.VMEM((cols, 2, quarter), f32),
                 pltpu.VMEM((cols - 1, 3, 8, quarter), f32),
@@ -303,7 +373,7 @@
                 pltpu.SemaphoreType.DMA((cols,)),
             ],
             compiler_params=pltpu.CompilerParams(
-                collective_id=0, has_side_effects=True, vmem_limit_bytes=32 << 20),
+                collective_id=0, has_side_effects=True, vmem_limit_bytes=60 << 20),
         )(psi0, onsite, hop_x, hop_y, cos_coef.T, sin_coef.T)
 
     placed = (P("col", "slab", None), P("slab", None), P("slab", None), P("slab", None), P(), P())

time: 38.8 us -> 31.7 us (0.82)
  local copies, waits for them, and re-layouts: 5.19 us -> 1.47 us
  Pallas kernels: 33.2 us -> 30 us
    unnamed x13 -> x1, local copies, waits for them, and re-layouts: 5.19 us -> 1.47 us
    pallas_call x1, Pallas kernels: 33.2 us -> 30 us  [on_device(): pl.pallas_call(functools.partial(kernel, slabs, cols), out_shape=jax.Shap...]
where the time goes in v1:
time: 31.7 us; the launch traced here: 31.5 us
  Pallas kernels  30 us (95%)
  local copies, waits for them, and re-layouts  1.47 us (5%)
    pallas_call x1, Pallas kernels, on_device(): pl.pallas_call(functools.partial(kernel, slabs, cols), out_shape=jax.Shap...  30 us
    unnamed x1, local copies, waits for them, and re-layouts  1.47 us

profile of v1, /device:TPU:7, one launch (start us, length us, event | category | flops | bytes accessed | tf_op | source)
XLA Modules:
  0.0 31.5 jit_solution(1210927391236580058)
XLA Ops:
  0.0 30.0 %shard_map.64 = f32[8,2,4,256]{3,2,1,0:T(4,128)} custom-call(bf16[64,4,1024]{2,1,0:T(4,128)(2,1)} %psi.1, f32[4,1024]{1,0:T(4,128)} %onsite_hbm.1, f32[4,1024]{1,0:T(4,128)} %hop_x_hbm.1, f32[4,1024]{1,0:T(4,128)} %hop_y_hbm.1, f32[3,8]{1,0:T(4,128)} %bitcast.2, f32[3,8]{1,0:T(4,128)} %bitcast.3), custom_call_target="tpu_custom_call" | custom-call | tf_op jit(solution)/shard_map/pallas_call | solution.py:338
  30.1 1.5 %copy.8 = f32[8,2,4,256]{3,2,1,0:T(4,128)} copy(f32[8,2,4,256]{3,2,1,0:T(4,128)} %shard_map.64) | data formatting | bytes 131072

commit v2 on v1

--- a/solution.py
+++ b/solution.py
@@ -10,12 +10,13 @@
 MESH = pl.DeviceIdType.MESH
 CHUNKS = 8
 LANES = 128
+AHEAD = 2
 
 
 def kernel(slabs, cols, psi, onsite_hbm, hop_x_hbm, hop_y_hbm, cos_hbm, sin_hbm, out,
            onsite, hop_x, hop_y, cos_ref, sin_ref, input_sem, field, to_up, to_down, from_down, from_up, coef, states, first, second, beside, acc, part, extra,
            got, got_extra, local_sem, send_sem, recv_sem, coef_send, coef_recv,
-           part_send, part_recv, extra_send, extra_recv):
+           part_send, part_recv, extra_send, extra_recv, go):
     slab = lax.axis_index("slab")
     col = lax.axis_index("col")
     batch, rows, width = psi.shape
@@ -50,6 +51,69 @@
         src_ref=to_down, dst_ref=from_up, send_sem=coef_send.at[1],
         recv_sem=coef_recv.at[1], device_id=(slab - 1, col), device_id_type=MESH)
 
+    place = lax.rem(slab, 4)
+    is_0, is_1, is_2, is_3 = (place == n for n in range(4))
+
+    def greet(sem_of, other):
+        for by in range(cols):
+            pl.semaphore_signal(sem_of, inc=1, device_id=(other, lax.rem(col + by, cols)),
+                                device_id_type=MESH)
+
+    barrier = pltpu.get_barrier_semaphore()
+
+    @pl.when((is_0 | is_1) & has_up)
+    def _():
+        greet(barrier, slab + 1)
+
+    @pl.when(jnp.logical_not(is_2) & has_down)
+    def _():
+        greet(barrier, slab - 1)
+
+    @pl.when(jnp.logical_not(is_3))
+    def _():
+        for by in range(1, cols):
+            pl.semaphore_signal(barrier, inc=1, device_id=(slab, lax.rem(col + by, cols)),
+                                device_id_type=MESH)
+
+    @pl.when(jnp.logical_not(is_3) | has_up)
+    def _():
+        pl.semaphore_wait(barrier, jnp.where(
+            is_3, cols, jnp.where(is_2, 3 * cols - 1, 2 * cols - 1)))
+
+    def send_up(chunks):
+        for i in chunks:
+            upward(i).start()
+
+    def send_down(chunks):
+        for i in chunks:
+            downward(i).start()
+
+    ready_up = jnp.logical_not(is_1) & has_up
+    ready_down = (is_1 | is_2) & has_down
+    asked_up = is_1 & has_up
+    asked_down = (is_0 | is_3) & has_down
+    asked = asked_up | asked_down
+
+    @pl.when(ready_up)
+    def _():
+        send_up(range(AHEAD))
+
+    @pl.when(ready_down)
+    def _():
+        send_down(range(AHEAD))
+
+    @pl.when(is_2 | (is_3 & has_up))
+    def _():
+        for by in range(cols):
+            pl.semaphore_signal(go.at[col], inc=1, device_id=(slab + 1, lax.rem(col + by, cols)),
+                                device_id_type=MESH)
+
+    @pl.when(is_2)
+    def _():
+        for by in range(cols):
+            pl.semaphore_signal(go.at[col], inc=1, device_id=(slab - 1, lax.rem(col + by, cols)),
+                                device_id_type=MESH)
+
     loads = [
         pltpu.make_async_copy(source, target, input_sem.at[n])
         for n, (source, target) in enumerate((
@@ -57,24 +121,6 @@
             (cos_hbm, cos_ref), (sin_hbm, sin_ref)))]
     for load in loads:
         load.start()
-    for i in range(CHUNKS):
-        local(i).start()
-
-    barrier = pltpu.get_barrier_semaphore()
-    for by in range(1, cols):
-        pl.semaphore_signal(barrier, inc=1, device_id=(slab, lax.rem(col + by, cols)),
-                            device_id_type=MESH)
-
-    @pl.when(has_up)
-    def _():
-        for other in range(cols):
-            pl.semaphore_signal(barrier, inc=1, device_id=(slab + 1, other), device_id_type=MESH)
-
-    @pl.when(has_down)
-    def _():
-        for other in range(cols):
-            pl.semaphore_signal(barrier, inc=1, device_id=(slab - 1, other), device_id_type=MESH)
-
     for load in loads:
         load.wait()
     zero = jnp.zeros((1, width), jnp.float32)
@@ -83,25 +129,19 @@
     to_down[...] = jnp.concatenate(
         [hop_x[0:1, :], onsite[0:1, :], hop_y[0:1, :], zero], axis=0)
 
-    sides = jnp.where(has_up, 1, 0) + jnp.where(has_down, 1, 0)
-    pl.semaphore_wait(barrier, cols - 1 + cols * sides)
-
-    @pl.when(has_up)
+    @pl.when(ready_up)
     def _():
         coef_up.start()
-
-    @pl.when(has_down)
+        send_up(range(AHEAD, CHUNKS))
+
+    @pl.when(ready_down)
     def _():
         coef_down.start()
+        send_down(range(AHEAD, CHUNKS))
 
     for i in range(CHUNKS):
-        @pl.when(has_up)
-        def _():
-            upward(i).start()
-
-        @pl.when(has_down)
-        def _():
-            downward(i).start()
+        local(i).start()
+
 
     blank = jnp.zeros((batch, 2, width), jnp.bfloat16)
 
@@ -116,6 +156,22 @@
         from_up[...] = jnp.zeros_like(from_up)
 
     acc[...] = jnp.zeros_like(acc)
+
+    @pl.when(asked)
+    def _():
+        pl.semaphore_wait(go.at[col], 1)
+
+    @pl.when(asked_up)
+    def _():
+        send_up(range(AHEAD))
+        coef_up.start()
+        send_up(range(AHEAD, CHUNKS))
+
+    @pl.when(asked_down)
+    def _():
+        send_down(range(AHEAD))
+        coef_down.start()
+        send_down(range(AHEAD, CHUNKS))
 
     @pl.when(has_down)
     def _():
@@ -232,10 +288,17 @@
 
     lax.fori_loop(0, CHUNKS, chunk, 0)
 
+    @pl.when(asked)
+    def _():
+        for by in range(1, cols):
+            pl.semaphore_wait(go.at[lax.rem(col + by, cols)], 1)
+
+    fold_row = lax.broadcasted_iota(jnp.int32, (8, quarter), 0)
+
     def folded(maps):
         size = 4
         while size:
-            upper = lax.rem(row_id // size, 2) == 1
+            upper = lax.rem(fold_row // size, 2) == 1
             half = len(maps) // 2
             maps = [
                 jnp.where(upper, maps[n + half] + pltpu.roll(maps[n + half], size, 0),
@@ -244,32 +307,30 @@
             size //= 2
         return maps[0]
 
-    whole = [folded([acc[8 * k + n] for n in range(8)]) for k in range(3)]
-    for k in range(3):
-        for j in range(cols):
-            part[j, k] = whole[k][:, j * quarter:(j + 1) * quarter]
-    two = jnp.concatenate([whole[1][6:7], whole[2][6:7]], axis=0)
-    for j in range(cols):
-        extra[j] = two[:, j * quarter:(j + 1) * quarter]
-
     def to_peer(by):
-        peer = lax.rem(col + by, cols)
         return pltpu.make_async_remote_copy(
-            src_ref=part.at[peer], dst_ref=got.at[by - 1], send_sem=part_send.at[by - 1],
-            recv_sem=part_recv.at[by - 1], device_id=(slab, peer), device_id_type=MESH)
+            src_ref=part.at[by], dst_ref=got.at[by - 1], send_sem=part_send.at[by - 1],
+            recv_sem=part_recv.at[by - 1], device_id=(slab, lax.rem(col + by, cols)),
+            device_id_type=MESH)
 
     def to_below(by):
-        peer = lax.rem(col + by, cols)
         return pltpu.make_async_remote_copy(
-            src_ref=extra.at[peer], dst_ref=got_extra.at[by], send_sem=extra_send.at[by],
-            recv_sem=extra_recv.at[by], device_id=(slab - 1, peer), device_id_type=MESH)
-
-    for by in range(1, cols):
-        to_peer(by).start()
-
-    @pl.when(has_down)
-    def _():
-        for by in range(cols):
+            src_ref=extra.at[by], dst_ref=got_extra.at[by], send_sem=extra_send.at[by],
+            recv_sem=extra_recv.at[by], device_id=(slab - 1, lax.rem(col + by, cols)),
+            device_id_type=MESH)
+
+    for by in (2, 1, 3, 0):
+        there = pl.ds(pl.multiple_of(lax.rem(col + by, cols) * quarter, quarter), quarter)
+        for k in range(3):
+            whole = folded([acc[8 * k + n, :, there] for n in range(8)])
+            part[by, k] = whole
+            if k:
+                extra[by, k - 1:k] = whole[6:7]
+        if by:
+            to_peer(by).start()
+
+        @pl.when(has_down)
+        def _():
             to_below(by).start()
 
     @pl.when(jnp.logical_not(has_up))
@@ -295,7 +356,7 @@
     along = []
     across = []
     for k in range(3):
-        total = part[col, k] + got[0, k] + got[1, k] + got[2, k]
+        total = part[0, k] + got[0, k] + got[1, k] + got[2, k]
         a = total[0:4]
         if k:
             a = a + jnp.where(row4 == 3, extra_sum[k - 1:k], 0.0)
@@ -371,10 +432,12 @@
                 pltpu.SemaphoreType.DMA((cols - 1,)),
                 pltpu.SemaphoreType.DMA((cols,)),
                 pltpu.SemaphoreType.DMA((cols,)),
+                pltpu.SemaphoreType.REGULAR((cols,)),
             ],
             compiler_params=pltpu.CompilerParams(
-                collective_id=0, has_side_effects=True, vmem_limit_bytes=60 << 20),
-        )(psi0, onsite, hop_x, hop_y, cos_coef.T, sin_coef.T)
+                collective_id=0, has_side_effects=True, vmem_limit_bytes=32 << 20),
+        )(*(pltpu.with_memory_space_constraint(a, pltpu.HBM) for a in (
+            psi0, onsite, hop_x, hop_y, cos_coef.T, sin_coef.T)))
 
     placed = (P("col", "slab", None), P("slab", None), P("slab", None), P("slab", None), P(), P())
     return jax.shard_map(

time: 31.7 us -> 27.7 us (0.87)
  the two profiles are of different devices: /device:TPU:7 before, /device:TPU:65 now
where the time goes in v2:
time: 27.7 us; the launch traced here: 27.5 us
  Pallas kernels  26.9 us (97%)
  local copies, waits for them, and re-layouts  0.63 us (2%)
    pallas_call x1, Pallas kernels, on_device(): pl.pallas_call(functools.partial(kernel, slabs, cols), out_shape=jax.Shap...  26.9 us
    unnamed x1, local copies, waits for them, and re-layouts  0.63 us

profile of v2, /device:TPU:65, one launch (start us, length us, event | category | flops | bytes accessed | tf_op | source)
XLA Modules:
  0.0 27.5 jit_solution(13914458951780987462)
XLA Ops:
  0.0 26.9 %shard_map.64 = f32[8,2,4,256]{3,2,1,0:T(4,128)S(1)} custom-call(bf16[64,4,1024]{2,1,0:T(4,128)(2,1)} %psi.1, f32[4,1024]{1,0:T(4,128)} %onsite_hbm.1, f32[4,1024]{1,0:T(4,128)} %hop_x_hbm.1, f32[4,1024]{1,0:T(4,128)} %hop_y_hbm.1, f32[3,8]{1,0:T(4,128)} %bitcast.2, f32[3,8]{1,0:T(4,128)} %bitcast.3), custom_call_target="tpu_custom_call" | custom-call | tf_op jit(solution)/shard_map/pallas_call | solution.py:399
  26.9 0.6 %copy.8 = f32[8,2,4,256]{3,2,1,0:T(4,128)} copy(f32[8,2,4,256]{3,2,1,0:T(4,128)S(1)} %shard_map.64) | data formatting | bytes 131072

commit v3 on v2

--- a/solution.py
+++ b/solution.py
@@ -14,7 +14,7 @@
 
 
 def kernel(slabs, cols, psi, onsite_hbm, hop_x_hbm, hop_y_hbm, cos_hbm, sin_hbm, out,
-           onsite, hop_x, hop_y, cos_ref, sin_ref, input_sem, field, to_up, to_down, from_down, from_up, coef, states, first, second, beside, acc, part, extra,
+           onsite, hop_x, hop_y, cos_ref, sin_ref, input_sem, field, to_up, to_down, from_down, from_up, coef, states, first, second, beside, acc, sums, kept, part, extra,
            got, got_extra, local_sem, send_sem, recv_sem, coef_send, coef_recv,
            part_send, part_recv, extra_send, extra_recv, go):
     slab = lax.axis_index("slab")
@@ -69,6 +69,10 @@
     def _():
         greet(barrier, slab - 1)
 
+    @pl.when(is_2)
+    def _():
+        pl.semaphore_signal(barrier, inc=1, device_id=(slab - 1, col), device_id_type=MESH)
+
     @pl.when(jnp.logical_not(is_3))
     def _():
         for by in range(1, cols):
@@ -78,7 +82,7 @@
     @pl.when(jnp.logical_not(is_3) | has_up)
     def _():
         pl.semaphore_wait(barrier, jnp.where(
-            is_3, cols, jnp.where(is_2, 3 * cols - 1, 2 * cols - 1)))
+            is_3, cols, jnp.where(is_2, 3 * cols - 1, jnp.where(is_1, 2 * cols, 2 * cols - 1))))
 
     def send_up(chunks):
         for i in chunks:
@@ -88,11 +92,9 @@
         for i in chunks:
             downward(i).start()
 
-    ready_up = jnp.logical_not(is_1) & has_up
+    ready_up = has_up
     ready_down = (is_1 | is_2) & has_down
-    asked_up = is_1 & has_up
-    asked_down = (is_0 | is_3) & has_down
-    asked = asked_up | asked_down
+    asked = (is_0 | is_3) & has_down
 
     @pl.when(ready_up)
     def _():
@@ -106,12 +108,6 @@
     def _():
         for by in range(cols):
             pl.semaphore_signal(go.at[col], inc=1, device_id=(slab + 1, lax.rem(col + by, cols)),
-                                device_id_type=MESH)
-
-    @pl.when(is_2)
-    def _():
-        for by in range(cols):
-            pl.semaphore_signal(go.at[col], inc=1, device_id=(slab - 1, lax.rem(col + by, cols)),
                                 device_id_type=MESH)
 
     loads = [
@@ -156,19 +152,11 @@
         from_up[...] = jnp.zeros_like(from_up)
 
     acc[...] = jnp.zeros_like(acc)
+    sums[...] = jnp.zeros_like(sums)
 
     @pl.when(asked)
     def _():
         pl.semaphore_wait(go.at[col], 1)
-
-    @pl.when(asked_up)
-    def _():
-        send_up(range(AHEAD))
-        coef_up.start()
-        send_up(range(AHEAD, CHUNKS))
-
-    @pl.when(asked_down)
-    def _():
         send_down(range(AHEAD))
         coef_down.start()
         send_down(range(AHEAD, CHUNKS))
@@ -218,10 +206,11 @@
     def rounded(f):
         return f.astype(jnp.bfloat16).astype(jnp.float32)
 
-    def mixed(f, g):
-        return jnp.concatenate([
-            jnp.where(even_lane, f[:, k * LANES:(k + 1) * LANES], g[:, k * LANES:(k + 1) * LANES])
-            for k in range(tiles)], axis=1)
+    def load_states(g, count):
+        for c in range(8):
+            block = field[g * 8 + c, 0:count, :].astype(jnp.float32)
+            for k in range(tiles):
+                states[k, 8 * c:8 * c + count, :] = block[:, k * LANES:(k + 1) * LANES]
 
     def p_row(x):
         return jnp.concatenate(
@@ -231,81 +220,82 @@
         return (coef[0, x + 2] * row(x) - coef[1, x + 1] * row(x - 1)
                 - coef[1, x + 2] * row(x + 1) - coef[2, x + 2] * side)
 
-    def q_row(x):
-        return first[x + 1]
-
-    def t_row(x):
-        return second[x]
-
-    def chunk(i, carry):
-        local(i).wait()
-
-        @pl.when(has_down)
-        def _():
-            upward(i).wait_recv()
-
-        @pl.when(has_up)
-        def _():
-            downward(i).wait_recv()
-
-        def group(j, inner):
-            for c in range(8):
-                block = field[i * per + j * 8 + c].astype(jnp.float32)
-                for k in range(tiles):
-                    states[k, 8 * c:8 * c + 8, :] = block[:, k * LANES:(k + 1) * LANES]
-            for x in range(-1, rows + 1):
-                side = partner(p_row(x), x)
-                if 0 <= x < rows:
-                    beside[0, x] = side
-                first[x + 1] = rounded(hamiltonian(p_row, x, side))
-            for x in range(rows):
-                side = partner(q_row(x), x)
-                beside[1, x] = side
-                t = rounded(2.0 * hamiltonian(q_row, x, side) - p_row(x))
-                second[x] = t
-                beside[2, x] = partner(t, x)
-            for x in range(rows):
-                acc[x] += p_row(x) * q_row(x + 1) - q_row(x) * p_row(x + 1)
-                if x < rows - 1:
-                    acc[8 + x] += p_row(x) * t_row(x + 1) - t_row(x) * p_row(x + 1)
-                    acc[16 + x] += q_row(x) * t_row(x + 1) - t_row(x) * q_row(x + 1)
-                else:
-                    acc[8 + x] -= t_row(x) * p_row(x + 1)
-                    acc[16 + x] -= t_row(x) * q_row(x + 1)
-            acc[14] += p_row(-1) * t_row(0)
-            acc[22] += q_row(-1) * t_row(0)
-            for h in range(rows // 2):
-                x = 2 * h
-                own = (mixed(p_row(x), p_row(x + 1)), mixed(q_row(x), q_row(x + 1)),
-                       mixed(t_row(x), t_row(x + 1)))
-                side = [mixed(beside[n, x], beside[n, x + 1]) for n in range(3)]
-                acc[4 + h] += own[0] * side[1] - own[1] * side[0]
-                acc[12 + h] += own[0] * side[2] - own[2] * side[0]
-                acc[20 + h] += own[1] * side[2] - own[2] * side[1]
-            return inner
-
-        return lax.fori_loop(0, per // 8, group, carry)
-
-    lax.fori_loop(0, CHUNKS, chunk, 0)
-
-    @pl.when(asked)
-    def _():
-        for by in range(1, cols):
-            pl.semaphore_wait(go.at[lax.rem(col + by, cols)], 1)
-
-    fold_row = lax.broadcasted_iota(jnp.int32, (8, quarter), 0)
-
-    def folded(maps):
-        size = 4
-        while size:
-            upper = lax.rem(fold_row // size, 2) == 1
-            half = len(maps) // 2
-            maps = [
-                jnp.where(upper, maps[n + half] + pltpu.roll(maps[n + half], size, 0),
-                          maps[n] + pltpu.roll(maps[n], 8 - size, 0))
-                for n in range(half)]
-            size //= 2
-        return maps[0]
+    def lower(g):
+        load_states(g, 6)
+        for x in range(-1, 2):
+            side = partner(p_row(x), x)
+            q = rounded(hamiltonian(p_row, x, side))
+            if x < 0:
+                first[0] = q
+            else:
+                kept[g, x] = q
+                kept[g, 3 + x] = side
+
+        def q_row(x):
+            return first[0] if x < 0 else kept[g, x]
+
+        side = partner(q_row(0), 0)
+        kept[g, 5] = side
+        t = rounded(2.0 * hamiltonian(q_row, 0, side) - p_row(0))
+        kept[g, 2] = t
+        sums[0] += p_row(-1) * t
+        sums[1] += q_row(-1) * t
+
+    def upper(g):
+        load_states(g, 8)
+
+        def q_row(x):
+            return kept[g, x] if x < 2 else first[x - 1]
+
+        beside[0, 0] = kept[g, 3]
+        beside[0, 1] = kept[g, 4]
+        beside[1, 0] = kept[g, 5]
+        second[0] = kept[g, 2]
+        beside[2, 0] = partner(kept[g, 2], 0)
+        for x in range(2, rows + 1):
+            side = partner(p_row(x), x)
+            if x < rows:
+                beside[0, x] = side
+            first[x - 1] = rounded(hamiltonian(p_row, x, side))
+        for x in range(1, rows):
+            side = partner(q_row(x), x)
+            beside[1, x] = side
+            t = rounded(2.0 * hamiltonian(q_row, x, side) - p_row(x))
+            second[x] = t
+            beside[2, x] = partner(t, x)
+
+    def products(g, tile):
+        lanes = pl.ds(pl.multiple_of(tile * LANES, LANES), LANES)
+
+        def p(x):
+            return states[tile, pl.ds(x + 2, 8, stride=8), :]
+
+        def q(x):
+            return kept[g, x, :, lanes] if x < 2 else first[x - 1, :, lanes]
+
+        def t(x):
+            return second[x, :, lanes]
+
+        def add(n, value):
+            acc[n, :, lanes] += value
+
+        for x in range(rows):
+            add(x, p(x) * q(x + 1) - q(x) * p(x + 1))
+            if x < rows - 1:
+                add(8 + x, p(x) * t(x + 1) - t(x) * p(x + 1))
+                add(16 + x, q(x) * t(x + 1) - t(x) * q(x + 1))
+            else:
+                add(8 + x, -t(x) * p(x + 1))
+                add(16 + x, -t(x) * q(x + 1))
+        for h in range(rows // 2):
+            x = 2 * h
+            own = [jnp.where(even_lane, row(x), row(x + 1)) for row in (p, q, t)]
+            side = [
+                jnp.where(even_lane, beside[n, x, :, lanes], beside[n, x + 1, :, lanes])
+                for n in range(3)]
+            add(4 + h, own[0] * side[1] - own[1] * side[0])
+            add(12 + h, own[0] * side[2] - own[2] * side[0])
+            add(20 + h, own[1] * side[2] - own[2] * side[1])
 
     def to_peer(by):
         return pltpu.make_async_remote_copy(
@@ -314,24 +304,97 @@
             device_id_type=MESH)
 
     def to_below(by):
+        peer = lax.rem(col + by, cols)
         return pltpu.make_async_remote_copy(
-            src_ref=extra.at[by], dst_ref=got_extra.at[by], send_sem=extra_send.at[by],
-            recv_sem=extra_recv.at[by], device_id=(slab - 1, lax.rem(col + by, cols)),
+            src_ref=extra.at[peer], dst_ref=got_extra.at[by], send_sem=extra_send.at[by],
+            recv_sem=extra_recv.at[by], device_id=(slab - 1, peer),
             device_id_type=MESH)
 
+    def wait_lower(i):
+        local(i).wait()
+
+        @pl.when(has_down)
+        def _():
+            upward(i).wait_recv()
+
+    def wait_upper(i):
+        @pl.when(has_up)
+        def _():
+            downward(i).wait_recv()
+
+    def send_extra():
+        @pl.when(asked)
+        def _():
+            for by in range(1, cols):
+                pl.semaphore_wait(go.at[lax.rem(col + by, cols)], 1)
+
+        @pl.when(has_down)
+        def _():
+            for n in range(2):
+                total = jnp.sum(sums[n], axis=0, keepdims=True)
+                for j in range(cols):
+                    extra[j, n:n + 1] = total[:, j * quarter:(j + 1) * quarter]
+            for by in (2, 1, 3, 0):
+                to_below(by).start()
+
+    @pl.when(jnp.logical_not(is_0))
+    def _():
+        def lower_chunk(i, carry):
+            wait_lower(i)
+            lower(i)
+            return carry
+
+        lax.fori_loop(0, CHUNKS, lower_chunk, 0)
+        send_extra()
+
+    def chunk(i):
+        @pl.when(is_0)
+        def _():
+            wait_lower(i)
+            lower(i)
+
+        wait_upper(i)
+        upper(i)
+
+    def whole_chunk(i, carry):
+        chunk(i)
+        for k in range(tiles):
+            products(i, k)
+        return carry
+
+    lax.fori_loop(0, CHUNKS - 1, whole_chunk, 0)
+    last = CHUNKS - 1
+    chunk(last)
+
+    fold_row = lax.broadcasted_iota(jnp.int32, (8, quarter), 0)
+
+    def folded(maps):
+        size = 4
+        while size:
+            upper_rows = lax.rem(fold_row // size, 2) == 1
+            half = len(maps) // 2
+            maps = [
+                jnp.where(upper_rows, maps[n + half] + pltpu.roll(maps[n + half], size, 0),
+                          maps[n] + pltpu.roll(maps[n], 8 - size, 0))
+                for n in range(half)]
+            size //= 2
+        return maps[0]
+
+    per_quarter = quarter // LANES
     for by in (2, 1, 3, 0):
-        there = pl.ds(pl.multiple_of(lax.rem(col + by, cols) * quarter, quarter), quarter)
+        peer = lax.rem(col + by, cols)
+        there = pl.ds(pl.multiple_of(peer * quarter, quarter), quarter)
+        for k in range(per_quarter):
+            products(last, peer * per_quarter + k)
         for k in range(3):
-            whole = folded([acc[8 * k + n, :, there] for n in range(8)])
-            part[by, k] = whole
-            if k:
-                extra[by, k - 1:k] = whole[6:7]
+            maps = [acc[8 * k + n, :, there] for n in range(6)]
+            part[by, k] = folded(maps + maps[4:6])
         if by:
             to_peer(by).start()
 
-        @pl.when(has_down)
-        def _():
-            to_below(by).start()
+    @pl.when(is_0)
+    def _():
+        send_extra()
 
     @pl.when(jnp.logical_not(has_up))
     def _():
@@ -419,6 +482,8 @@
                 pltpu.VMEM((rows, 8, width), f32),
                 pltpu.VMEM((3, rows, 8, width), f32),
                 pltpu.VMEM((24, 8, width), f32),
+                pltpu.VMEM((2, 8, width), f32),
+                pltpu.VMEM((CHUNKS, 6, 8, width), f32),
                 pltpu.VMEM((cols, 3, 8, quarter), f32),
                 pltpu.VMEM((cols, 2, quarter), f32),
                 pltpu.VMEM((cols - 1, 3, 8, quarter), f32),

time: 27.7 us -> 27.1 us (0.978)
  the two profiles are of different devices: /device:TPU:65 before, /device:TPU:7 now
where the time goes in v3:
time: 27.1 us; the launch traced here: 27 us
  Pallas kernels  26.3 us (97%)
  local copies, waits for them, and re-layouts  0.63 us (2%)
    pallas_call x1, Pallas kernels, on_device(): pl.pallas_call(functools.partial(kernel, slabs, cols), out_shape=jax.Shap...  26.3 us
    unnamed x1, local copies, waits for them, and re-layouts  0.63 us

profile of v3, /device:TPU:7, one launch (start us, length us, event | category | flops | bytes accessed | tf_op | source)
XLA Modules:
  0.0 27.0 jit_solution(14213338357764132063)
XLA Ops:
  0.0 26.3 %shard_map.64 = f32[8,2,4,256]{3,2,1,0:T(4,128)S(1)} custom-call(bf16[64,4,1024]{2,1,0:T(4,128)(2,1)} %psi.1, f32[4,1024]{1,0:T(4,128)} %onsite_hbm.1, f32[4,1024]{1,0:T(4,128)} %hop_x_hbm.1, f32[4,1024]{1,0:T(4,128)} %hop_y_hbm.1, f32[3,8]{1,0:T(4,128)} %bitcast.2, f32[3,8]{1,0:T(4,128)} %bitcast.3), custom_call_target="tpu_custom_call" | custom-call | tf_op jit(solution)/shard_map/pallas_call | solution.py:462
  26.3 0.6 %copy.8 = f32[8,2,4,256]{3,2,1,0:T(4,128)} copy(f32[8,2,4,256]{3,2,1,0:T(4,128)S(1)} %shard_map.64) | data formatting | bytes 131072

commit v4 on v3

--- a/solution.py
+++ b/solution.py
@@ -14,7 +14,7 @@
 
 
 def kernel(slabs, cols, psi, onsite_hbm, hop_x_hbm, hop_y_hbm, cos_hbm, sin_hbm, out,
-           onsite, hop_x, hop_y, cos_ref, sin_ref, input_sem, field, to_up, to_down, from_down, from_up, coef, states, first, second, beside, acc, sums, kept, part, extra,
+           onsite, hop_x, hop_y, cos_ref, sin_ref, input_sem, field, to_up, to_down, from_down, from_up, coef, states, first, second, beside, acc, sums, part, extra,
            got, got_extra, local_sem, send_sem, recv_sem, coef_send, coef_recv,
            part_send, part_recv, extra_send, extra_recv, go):
     slab = lax.axis_index("slab")
@@ -206,11 +206,11 @@
     def rounded(f):
         return f.astype(jnp.bfloat16).astype(jnp.float32)
 
-    def load_states(g, count):
+    def load_states(g, start, stop):
         for c in range(8):
-            block = field[g * 8 + c, 0:count, :].astype(jnp.float32)
+            block = field[g * 8 + c, start:stop, :].astype(jnp.float32)
             for k in range(tiles):
-                states[k, 8 * c:8 * c + count, :] = block[:, k * LANES:(k + 1) * LANES]
+                states[k, 8 * c + start:8 * c + stop, :] = block[:, k * LANES:(k + 1) * LANES]
 
     def p_row(x):
         return jnp.concatenate(
@@ -220,58 +220,39 @@
         return (coef[0, x + 2] * row(x) - coef[1, x + 1] * row(x - 1)
                 - coef[1, x + 2] * row(x + 1) - coef[2, x + 2] * side)
 
-    def lower(g):
-        load_states(g, 6)
-        for x in range(-1, 2):
+    def vectors(g, start, stop, row_range, t_range):
+        load_states(g, start, stop)
+        for x in row_range:
             side = partner(p_row(x), x)
-            q = rounded(hamiltonian(p_row, x, side))
-            if x < 0:
-                first[0] = q
-            else:
-                kept[g, x] = q
-                kept[g, 3 + x] = side
-
-        def q_row(x):
-            return first[0] if x < 0 else kept[g, x]
-
-        side = partner(q_row(0), 0)
-        kept[g, 5] = side
-        t = rounded(2.0 * hamiltonian(q_row, 0, side) - p_row(0))
-        kept[g, 2] = t
-        sums[0] += p_row(-1) * t
-        sums[1] += q_row(-1) * t
-
-    def upper(g):
-        load_states(g, 8)
-
-        def q_row(x):
-            return kept[g, x] if x < 2 else first[x - 1]
-
-        beside[0, 0] = kept[g, 3]
-        beside[0, 1] = kept[g, 4]
-        beside[1, 0] = kept[g, 5]
-        second[0] = kept[g, 2]
-        beside[2, 0] = partner(kept[g, 2], 0)
-        for x in range(2, rows + 1):
-            side = partner(p_row(x), x)
-            if x < rows:
+            if x in t_range:
                 beside[0, x] = side
-            first[x - 1] = rounded(hamiltonian(p_row, x, side))
-        for x in range(1, rows):
+            first[x + 1] = rounded(hamiltonian(p_row, x, side))
+        for x in t_range:
             side = partner(q_row(x), x)
             beside[1, x] = side
             t = rounded(2.0 * hamiltonian(q_row, x, side) - p_row(x))
             second[x] = t
             beside[2, x] = partner(t, x)
 
-    def products(g, tile):
+    def q_row(x):
+        return first[x + 1]
+
+    def lower_vectors(g):
+        vectors(g, 0, 6, range(-1, 3), range(0, 2))
+        sums[0] += p_row(-1) * second[0]
+        sums[1] += q_row(-1) * second[0]
+
+    def upper_vectors(g):
+        vectors(g, 2, 8, range(1, rows + 1), range(2, rows))
+
+    def rows_at(tile):
         lanes = pl.ds(pl.multiple_of(tile * LANES, LANES), LANES)
 
         def p(x):
             return states[tile, pl.ds(x + 2, 8, stride=8), :]
 
         def q(x):
-            return kept[g, x, :, lanes] if x < 2 else first[x - 1, :, lanes]
+            return first[x + 1, :, lanes]
 
         def t(x):
             return second[x, :, lanes]
@@ -279,23 +260,39 @@
         def add(n, value):
             acc[n, :, lanes] += value
 
-        for x in range(rows):
-            add(x, p(x) * q(x + 1) - q(x) * p(x + 1))
-            if x < rows - 1:
-                add(8 + x, p(x) * t(x + 1) - t(x) * p(x + 1))
-                add(16 + x, q(x) * t(x + 1) - t(x) * q(x + 1))
-            else:
-                add(8 + x, -t(x) * p(x + 1))
-                add(16 + x, -t(x) * q(x + 1))
-        for h in range(rows // 2):
+        def across(h):
             x = 2 * h
             own = [jnp.where(even_lane, row(x), row(x + 1)) for row in (p, q, t)]
             side = [
                 jnp.where(even_lane, beside[n, x, :, lanes], beside[n, x + 1, :, lanes])
                 for n in range(3)]
-            add(4 + h, own[0] * side[1] - own[1] * side[0])
-            add(12 + h, own[0] * side[2] - own[2] * side[0])
-            add(20 + h, own[1] * side[2] - own[2] * side[1])
+            add(12 + h, own[0] * side[1] - own[1] * side[0])
+            add(14 + h, own[0] * side[2] - own[2] * side[0])
+            add(16 + h, own[1] * side[2] - own[2] * side[1])
+
+        return p, q, t, add, across
+
+    def lower_products(tile):
+        p, q, t, add, across = rows_at(tile)
+        for x in range(2):
+            add(x, p(x) * q(x + 1) - q(x) * p(x + 1))
+        add(4, p(0) * t(1) - t(0) * p(1))
+        add(8, q(0) * t(1) - t(0) * q(1))
+        add(5, -t(1) * p(2))
+        add(9, -t(1) * q(2))
+        across(0)
+
+    def upper_products(tile):
+        p, q, t, add, across = rows_at(tile)
+        for x in range(2, 4):
+            add(x, p(x) * q(x + 1) - q(x) * p(x + 1))
+        add(5, p(1) * t(2))
+        add(9, q(1) * t(2))
+        add(6, p(2) * t(3) - t(2) * p(3))
+        add(10, q(2) * t(3) - t(2) * q(3))
+        add(7, -t(3) * p(4))
+        add(11, -t(3) * q(4))
+        across(1)
 
     def to_peer(by):
         return pltpu.make_async_remote_copy(
@@ -311,8 +308,6 @@
             device_id_type=MESH)
 
     def wait_lower(i):
-        local(i).wait()
-
         @pl.when(has_down)
         def _():
             upward(i).wait_recv()
@@ -336,35 +331,6 @@
                     extra[j, n:n + 1] = total[:, j * quarter:(j + 1) * quarter]
             for by in (2, 1, 3, 0):
                 to_below(by).start()
-
-    @pl.when(jnp.logical_not(is_0))
-    def _():
-        def lower_chunk(i, carry):
-            wait_lower(i)
-            lower(i)
-            return carry
-
-        lax.fori_loop(0, CHUNKS, lower_chunk, 0)
-        send_extra()
-
-    def chunk(i):
-        @pl.when(is_0)
-        def _():
-            wait_lower(i)
-            lower(i)
-
-        wait_upper(i)
-        upper(i)
-
-    def whole_chunk(i, carry):
-        chunk(i)
-        for k in range(tiles):
-            products(i, k)
-        return carry
-
-    lax.fori_loop(0, CHUNKS - 1, whole_chunk, 0)
-    last = CHUNKS - 1
-    chunk(last)
 
     fold_row = lax.broadcasted_iota(jnp.int32, (8, quarter), 0)
 
@@ -381,20 +347,64 @@
         return maps[0]
 
     per_quarter = quarter // LANES
-    for by in (2, 1, 3, 0):
-        peer = lax.rem(col + by, cols)
-        there = pl.ds(pl.multiple_of(peer * quarter, quarter), quarter)
-        for k in range(per_quarter):
-            products(last, peer * per_quarter + k)
-        for k in range(3):
-            maps = [acc[8 * k + n, :, there] for n in range(6)]
-            part[by, k] = folded(maps + maps[4:6])
-        if by:
-            to_peer(by).start()
+
+    def share_out(products):
+        odd = lax.rem(col, 2)
+        for by in (2, 3 - 2 * odd, 1 + 2 * odd, 0):
+            peer = lax.rem(col + by, cols)
+            there = pl.ds(pl.multiple_of(peer * quarter, quarter), quarter)
+            for k in range(per_quarter):
+                products(peer * per_quarter + k)
+            maps = [acc[n, :, there] for n in range(18)]
+            part[by, 0:8] = folded(maps[0:8])
+            part[by, 8:16] = folded(maps[8:16])
+            part[by, 16:18] = folded(maps[16:18] * 4)[0:2]
+            if not (isinstance(by, int) and by == 0):
+                to_peer(by).start()
+
+    def lower_chunk(i):
+        wait_lower(i)
+        lower_vectors(i)
+        for k in range(tiles):
+            lower_products(k)
+
+    def upper_chunk(i):
+        wait_upper(i)
+        upper_vectors(i)
+        for k in range(tiles):
+            upper_products(k)
+
+    def sweep(count, *steps):
+        def step(i, carry):
+            for one in steps:
+                one(i)
+            return carry
+
+        lax.fori_loop(0, count, step, 0)
+
+    def here_now(i):
+        local(i).wait()
+
+    last = CHUNKS - 1
 
     @pl.when(is_0)
     def _():
+        here_now(0)
+        upper_chunk(0)
+        sweep(last, lambda i: here_now(i + 1), lambda i: upper_chunk(i + 1), lower_chunk)
+        wait_lower(last)
+        lower_vectors(last)
+        share_out(lower_products)
         send_extra()
+
+    @pl.when(jnp.logical_not(is_0))
+    def _():
+        sweep(CHUNKS, here_now, lower_chunk)
+        send_extra()
+        sweep(last, upper_chunk)
+        wait_upper(last)
+        upper_vectors(last)
+        share_out(upper_products)
 
     @pl.when(jnp.logical_not(has_up))
     def _():
@@ -418,13 +428,15 @@
     own_y = jnp.where(keep, own_y, 0.0)
     along = []
     across = []
+    total = part[0] + got[0] + got[1] + got[2]
     for k in range(3):
-        total = part[0, k] + got[0, k] + got[1, k] + got[2, k]
-        a = total[0:4]
+        a = total[4 * k:4 * k + 4]
         if k:
             a = a + jnp.where(row4 == 3, extra_sum[k - 1:k], 0.0)
         along.append(a * own_x)
-        across.append(jnp.concatenate([total[4:5], total[4:5], total[5:6], total[5:6]], axis=0) * own_y)
+        n = 12 + 2 * k
+        b = jnp.where(row4 < 2, total[n:n + 1], total[n + 1:n + 2])
+        across.append(b * own_y)
     for e in range(cos_ref.shape[1]):
         c0, c1, c2 = (cos_ref[n, e] for n in range(3))
         s0, s1, s2 = (sin_ref[n, e] for n in range(3))
@@ -481,12 +493,11 @@
                 pltpu.VMEM((rows + 2, 8, width), f32),
                 pltpu.VMEM((rows, 8, width), f32),
                 pltpu.VMEM((3, rows, 8, width), f32),
-                pltpu.VMEM((24, 8, width), f32),
+                pltpu.VMEM((18, 8, width), f32),
                 pltpu.VMEM((2, 8, width), f32),
-                pltpu.VMEM((CHUNKS, 6, 8, width), f32),
-                pltpu.VMEM((cols, 3, 8, quarter), f32),
+                pltpu.VMEM((cols, 18, quarter), f32),
                 pltpu.VMEM((cols, 2, quarter), f32),
-                pltpu.VMEM((cols - 1, 3, 8, quarter), f32),
+                pltpu.VMEM((cols - 1, 18, quarter), f32),
                 pltpu.VMEM((cols, 2, quarter), f32),
                 pltpu.SemaphoreType.DMA((CHUNKS,)),
                 pltpu.SemaphoreType.DMA((2, CHUNKS)),

time: 27.1 us -> 26.8 us (0.989)
  Pallas kernels: 26.3 us -> 25.9 us
    pallas_call x1, Pallas kernels: 26.3 us -> 25.9 us  [on_device(): pl.pallas_call(functools.partial(kernel, slabs, cols), out_shape=jax.Shap...]
where the time goes in v4:
time: 26.8 us; the launch traced here: 26.6 us
  Pallas kernels  25.9 us (97%)
  local copies, waits for them, and re-layouts  0.63 us (2%)
    pallas_call x1, Pallas kernels, on_device(): pl.pallas_call(functools.partial(kernel, slabs, cols), out_shape=jax.Shap...  25.9 us
    unnamed x1, local copies, waits for them, and re-layouts  0.63 us

profile of v4, /device:TPU:7, one launch (start us, length us, event | category | flops | bytes accessed | tf_op | source)
XLA Modules:
  0.0 26.6 jit_solution(17719616776966492269)
XLA Ops:
  0.0 25.9 %shard_map.64 = f32[8,2,4,256]{3,2,1,0:T(4,128)S(1)} custom-call(bf16[64,4,1024]{2,1,0:T(4,128)(2,1)} %psi.1, f32[4,1024]{1,0:T(4,128)} %onsite_hbm.1, f32[4,1024]{1,0:T(4,128)} %hop_x_hbm.1, f32[4,1024]{1,0:T(4,128)} %hop_y_hbm.1, f32[3,8]{1,0:T(4,128)} %bitcast.2, f32[3,8]{1,0:T(4,128)} %bitcast.3), custom_call_target="tpu_custom_call" | custom-call | tf_op jit(solution)/shard_map/pallas_call | solution.py:474
  26.0 0.6 %copy.8 = f32[8,2,4,256]{3,2,1,0:T(4,128)} copy(f32[8,2,4,256]{3,2,1,0:T(4,128)S(1)} %shard_map.64) | data formatting | bytes 131072

commit v5 on v4

--- a/solution.py
+++ b/solution.py
@@ -14,7 +14,7 @@
 
 
 def kernel(slabs, cols, psi, onsite_hbm, hop_x_hbm, hop_y_hbm, cos_hbm, sin_hbm, out,
-           onsite, hop_x, hop_y, cos_ref, sin_ref, input_sem, field, to_up, to_down, from_down, from_up, coef, states, first, second, beside, acc, sums, part, extra,
+           onsite, hop_x, hop_y, cos_ref, sin_ref, input_sem, field, to_up, to_down, from_down, from_up, coef, states, first, second, beside, acc, sums, kept, part, extra,
            got, got_extra, local_sem, send_sem, recv_sem, coef_send, coef_recv,
            part_send, part_recv, extra_send, extra_recv, go):
     slab = lax.axis_index("slab")
@@ -220,13 +220,23 @@
         return (coef[0, x + 2] * row(x) - coef[1, x + 1] * row(x - 1)
                 - coef[1, x + 2] * row(x + 1) - coef[2, x + 2] * side)
 
-    def vectors(g, start, stop, row_range, t_range):
+    def vectors(g, start, stop, row_range, t_range, again):
         load_states(g, start, stop)
         for x in row_range:
+            if again and x in (1, 2):
+                first[x + 1] = kept[g, x - 1]
+                if x in t_range:
+                    beside[0, x] = kept[g, 2]
+                continue
             side = partner(p_row(x), x)
+            q = rounded(hamiltonian(p_row, x, side))
+            first[x + 1] = q
             if x in t_range:
                 beside[0, x] = side
-            first[x + 1] = rounded(hamiltonian(p_row, x, side))
+            if x in (1, 2):
+                kept[g, x - 1] = q
+                if x not in t_range:
+                    kept[g, 2] = side
         for x in t_range:
             side = partner(q_row(x), x)
             beside[1, x] = side
@@ -237,13 +247,13 @@
     def q_row(x):
         return first[x + 1]
 
-    def lower_vectors(g):
-        vectors(g, 0, 6, range(-1, 3), range(0, 2))
+    def lower_vectors(g, again):
+        vectors(g, 0, 6, range(-1, 3), range(0, 2), again)
         sums[0] += p_row(-1) * second[0]
         sums[1] += q_row(-1) * second[0]
 
-    def upper_vectors(g):
-        vectors(g, 2, 8, range(1, rows + 1), range(2, rows))
+    def upper_vectors(g, again):
+        vectors(g, 2, 8, range(1, rows + 1), range(2, rows), again)
 
     def rows_at(tile):
         lanes = pl.ds(pl.multiple_of(tile * LANES, LANES), LANES)
@@ -350,7 +360,7 @@
 
     def share_out(products):
         odd = lax.rem(col, 2)
-        for by in (2, 3 - 2 * odd, 1 + 2 * odd, 0):
+        for by in (3 - odd, 2 - odd, 1 + 2 * odd, 0):
             peer = lax.rem(col + by, cols)
             there = pl.ds(pl.multiple_of(peer * quarter, quarter), quarter)
             for k in range(per_quarter):
@@ -362,15 +372,15 @@
             if not (isinstance(by, int) and by == 0):
                 to_peer(by).start()
 
-    def lower_chunk(i):
+    def lower_chunk(i, again):
         wait_lower(i)
-        lower_vectors(i)
+        lower_vectors(i, again)
         for k in range(tiles):
             lower_products(k)
 
-    def upper_chunk(i):
+    def upper_chunk(i, again):
         wait_upper(i)
-        upper_vectors(i)
+        upper_vectors(i, again)
         for k in range(tiles):
             upper_products(k)
 
@@ -390,20 +400,21 @@
     @pl.when(is_0)
     def _():
         here_now(0)
-        upper_chunk(0)
-        sweep(last, lambda i: here_now(i + 1), lambda i: upper_chunk(i + 1), lower_chunk)
+        upper_chunk(0, False)
+        sweep(last, lambda i: here_now(i + 1), lambda i: upper_chunk(i + 1, False),
+              lambda i: lower_chunk(i, True))
         wait_lower(last)
-        lower_vectors(last)
+        lower_vectors(last, True)
         share_out(lower_products)
         send_extra()
 
     @pl.when(jnp.logical_not(is_0))
     def _():
-        sweep(CHUNKS, here_now, lower_chunk)
+        sweep(CHUNKS, here_now, lambda i: lower_chunk(i, False))
         send_extra()
-        sweep(last, upper_chunk)
+        sweep(last, lambda i: upper_chunk(i, True))
         wait_upper(last)
-        upper_vectors(last)
+        upper_vectors(last, True)
         share_out(upper_products)
 
     @pl.when(jnp.logical_not(has_up))
@@ -495,6 +506,7 @@
                 pltpu.VMEM((3, rows, 8, width), f32),
                 pltpu.VMEM((18, 8, width), f32),
                 pltpu.VMEM((2, 8, width), f32),
+                pltpu.VMEM((CHUNKS, 3, 8, width), f32),
                 pltpu.VMEM((cols, 18, quarter), f32),
                 pltpu.VMEM((cols, 2, quarter), f32),
                 pltpu.VMEM((cols - 1, 18, quarter), f32),

time: 26.8 us -> 26.7 us (level)
  Pallas kernels: 25.9 us -> 25.6 us
    pallas_call x1, Pallas kernels: 25.9 us -> 25.6 us  [on_device(): pl.pallas_call(functools.partial(kernel, slabs, cols), out_shape=jax.Shap...]
where the time goes in v5:
time: 26.7 us; the launch traced here: 26.3 us
  Pallas kernels  25.6 us (96%)
  local copies, waits for them, and re-layouts  0.63 us (2%)
    pallas_call x1, Pallas kernels, on_device(): pl.pallas_call(functools.partial(kernel, slabs, cols), out_shape=jax.Shap...  25.6 us
    unnamed x1, local copies, waits for them, and re-layouts  0.63 us

profile of v5, /device:TPU:7, one launch (start us, length us, event | category | flops | bytes accessed | tf_op | source)
XLA Modules:
  0.0 26.3 jit_solution(8815908836169231200)
XLA Ops:
  0.0 25.6 %shard_map.64 = f32[8,2,4,256]{3,2,1,0:T(4,128)S(1)} custom-call(bf16[64,4,1024]{2,1,0:T(4,128)(2,1)} %psi.1, f32[4,1024]{1,0:T(4,128)} %onsite_hbm.1, f32[4,1024]{1,0:T(4,128)} %hop_x_hbm.1, f32[4,1024]{1,0:T(4,128)} %hop_y_hbm.1, f32[3,8]{1,0:T(4,128)} %bitcast.2, f32[3,8]{1,0:T(4,128)} %bitcast.3), custom_call_target="tpu_custom_call" | custom-call | tf_op jit(solution)/shard_map/pallas_call | solution.py:485
  25.6 0.6 %copy.8 = f32[8,2,4,256]{3,2,1,0:T(4,128)} copy(f32[8,2,4,256]{3,2,1,0:T(4,128)S(1)} %shard_map.64) | data formatting | bytes 131072

commit v6 on v5

--- a/solution.py
+++ b/solution.py
@@ -10,7 +10,7 @@
 MESH = pl.DeviceIdType.MESH
 CHUNKS = 8
 LANES = 128
-AHEAD = 2
+AHEAD = 1
 
 
 def kernel(slabs, cols, psi, onsite_hbm, hop_x_hbm, hop_y_hbm, cos_hbm, sin_hbm, out,

time: 26.7 us -> 26.8 us (level)
  no operation moved by 1% of the time
where the time goes in v6:
time: 26.8 us; the launch traced here: 26.4 us
  Pallas kernels  25.7 us (96%)
  local copies, waits for them, and re-layouts  0.63 us (2%)
    pallas_call x1, Pallas kernels, on_device(): pl.pallas_call(functools.partial(kernel, slabs, cols), out_shape=jax.Shap...  25.7 us
    unnamed x1, local copies, waits for them, and re-layouts  0.63 us

profile of v6, /device:TPU:7, one launch (start us, length us, event | category | flops | bytes accessed | tf_op | source)
XLA Modules:
  0.0 26.4 jit_solution(6668969544302056983)
XLA Ops:
  0.0 25.7 %shard_map.64 = f32[8,2,4,256]{3,2,1,0:T(4,128)S(1)} custom-call(bf16[64,4,1024]{2,1,0:T(4,128)(2,1)} %psi.1, f32[4,1024]{1,0:T(4,128)} %onsite_hbm.1, f32[4,1024]{1,0:T(4,128)} %hop_x_hbm.1, f32[4,1024]{1,0:T(4,128)} %hop_y_hbm.1, f32[3,8]{1,0:T(4,128)} %bitcast.2, f32[3,8]{1,0:T(4,128)} %bitcast.3), custom_call_target="tpu_custom_call" | custom-call | tf_op jit(solution)/shard_map/pallas_call | solution.py:485
  25.7 0.6 %copy.8 = f32[8,2,4,256]{3,2,1,0:T(4,128)} copy(f32[8,2,4,256]{3,2,1,0:T(4,128)S(1)} %shard_map.64) | data formatting | bytes 131072
